TPU v7x, 512 devices: a whole 4x4x16 slice. The times are simulated.
512 devices in a mesh: row: 32 (over z, y_lo), col: 16 (over y_hi, x, core).
Axes of the slice: x: 4, y: 4 (y_hi: 2, y_lo: 2; y = y_hi * 2 + y_lo), z: 16, core: 2. Of those that a mesh axis runs over, the one named last changes fastest.
Arguments:
- atom_feats: bfloat16 [32768, 128], P(('row', 'col')), may hold values from -6 to 6
- key_starts: int32 [1024], P(('row', 'col')), may hold values from -64 to 32704, as said below
- atom_counts: int32 [2048], replicated, may hold values from 8 to 24, as said below
- atom_gain: float32 [128], replicated, may hold values from 0.1 to 1.9
- w_query: bfloat16 [128, 128], replicated, may hold values from -0.5 to 0.5
- w_key: bfloat16 [128, 128], replicated, may hold values from -0.5 to 0.5
- w_value: bfloat16 [128, 128], replicated, may hold values from -0.5 to 0.5
- w_out: bfloat16 [128, 128], replicated, may hold values from -0.5 to 0.5
- w_pool: bfloat16 [128, 384], replicated, may hold values from -0.5 to 0.5
- w_back: bfloat16 [384, 128], replicated, may hold values from -0.3125 to 0.3125
- pair_state: bfloat16 [2048, 2048, 128], P('row', 'col'), may hold values from -6 to 6
- w_left: bfloat16 [384, 32], replicated, may hold values from -0.3125 to 0.3125
- w_right: bfloat16 [384, 32], replicated, may hold values from -0.3125 to 0.3125
- w_outer: bfloat16 [32, 32, 128], replicated, may hold values from -0.1875 to 0.1875
- pair_gain: float32 [128], replicated, may hold values from 0.1 to 1.9
- w_gate: bfloat16 [128, 512], replicated, may hold values from -0.5 to 0.5
- w_lift: bfloat16 [128, 512], replicated, may hold values from -0.5 to 0.5
- w_drop: bfloat16 [512, 128], replicated, may hold values from -0.25 to 0.25
Outputs:
- atom_out: bfloat16 [32768, 128], P(('row', 'col'))
- token_single: bfloat16 [2048, 384], P(('row', 'col'))
- pair_out: bfloat16 [2048, 2048, 128], P('row', 'col')
Inputs may be any that keep to these rules, and one draw needn't show every extreme that they name: key_starts[b] = 32 * b - 64 + offset, with offset a whole number from 0 to 32; the offset is 0 for the first block and 32 for the last. `atom_counts`: the counts sum to 32768.
All inputs are finite; a program needn't handle non-finite values.
Results may differ from a plain program's by a relative error of at most 0.007.
Values may be sent and summed in bfloat16 or wider, within the bound.
A program may use at most 64 MiB of HBM per device.

v0:
```python
import math
import jax
import jax.numpy as jnp
from jax import lax
from jax.sharding import PartitionSpec as P

HEADS = 4
QB = 32
KW = 128
FEWEST = 8
MOST = 24
EPSILON = 1e-05
BOTH = ("row", "col")


def shifted(block, distance):
    count = lax.axis_size(BOTH)
    route = [(i - distance, i) for i in range(count) if 0 <= i - distance < count]
    return lax.ppermute(block, BOTH, route)


def layer_norm(values, gain):
    mean_value = jnp.mean(values, axis=-1, keepdims=True)
    centred = values - mean_value
    variance = jnp.mean(centred * centred, axis=-1, keepdims=True)
    return centred * lax.rsqrt(variance + EPSILON) * gain


def project(source, weight):
    return jnp.dot(source, weight, preferred_element_type=jnp.float32).astype(jnp.bfloat16)


def atom_part(
    ext,
    feats_q,
    starts,
    first_atom,
    total_atoms,
    spans,
    atom_gain,
    w_query,
    w_key,
    w_value,
    w_out,
    w_pool,
    w_back,
):
    width = ext.shape[1]
    head = width // HEADS
    normed = layer_norm(ext.astype(jnp.float32), atom_gain).astype(jnp.bfloat16)
    keys = project(normed, w_key)
    values = project(normed, w_value)
    queries = project(normed[64:192], w_query)
    key_atom = first_atom - 96 + lax.broadcasted_iota(jnp.int32, (128, 256), 1)
    mask = (
        (key_atom >= starts) & (key_atom < starts + KW) & (key_atom >= 0) & (key_atom < total_atoms)
    )
    query_atom = first_atom - 32 + lax.broadcasted_iota(jnp.int32, (128, 1), 0)
    real = (query_atom >= 0) & (query_atom < total_atoms)
    pieces = []
    for h in range(HEADS):
        cut = slice(h * head, (h + 1) * head)
        scores = lax.dot_general(
            queries[:, cut],
            keys[:, cut],
            (((1,), (1,)), ((), ())),
            preferred_element_type=jnp.float32,
        ) * head ** (-0.5)
        raised = jnp.where(mask, jnp.exp(scores), 0.0)
        total = jnp.where(real, jnp.sum(raised, axis=-1, keepdims=True), 1.0)
        weights = (raised / total).astype(jnp.bfloat16)
        pieces.append(jnp.dot(weights, values[:, cut], preferred_element_type=jnp.float32))
    attended = jnp.concatenate(pieces, axis=1).astype(jnp.bfloat16)
    updated = (
        feats_q.astype(jnp.float32) + jnp.dot(attended, w_out, preferred_element_type=jnp.float32)
    ).astype(jnp.bfloat16)
    feature = jax.nn.relu(jnp.dot(updated, w_pool, preferred_element_type=jnp.float32)).astype(
        jnp.bfloat16
    )
    low, high = spans
    atoms = first_atom - 32 + lax.broadcasted_iota(jnp.int32, (low.shape[0], 128), 1)
    member = ((atoms >= low) & (atoms < high)).astype(jnp.bfloat16)
    pooled = jnp.dot(member, feature, preferred_element_type=jnp.float32)
    counts = jnp.maximum(high - low, 1).astype(jnp.float32)
    single = (pooled / counts).astype(jnp.bfloat16)
    back = project(single, w_back)
    lifted = lax.dot_general(
        member[:, 32:96], back, (((0,), (0,)), ((), ())), preferred_element_type=jnp.float32
    )
    atom_out = (updated[32:96].astype(jnp.float32) + lifted).astype(jnp.bfloat16)
    return (atom_out, single)


def per_device(
    atom_feats,
    key_starts,
    atom_counts,
    atom_gain,
    w_query,
    w_key,
    w_value,
    w_out,
    w_pool,
    w_back,
    pair_state,
    w_left,
    w_right,
    w_outer,
    pair_gain,
    w_gate,
    w_lift,
    w_drop,
):
    atom_rows, atom_width = atom_feats.shape
    devices = lax.axis_size(BOTH)
    rows, cols = (lax.axis_size("row"), lax.axis_size("col"))
    row, col = (lax.axis_index("row"), lax.axis_index("col"))
    position = row * cols + col
    total_atoms = atom_rows * devices
    total_tokens = atom_counts.shape[0]
    first_atom = position * atom_rows
    blocks = atom_rows // QB
    offsets = key_starts - (
        QB * (position * blocks + jnp.arange(blocks, dtype=jnp.int32)) - KW // 2
    )
    offset_rows = (
        jnp.zeros((8, atom_width), jnp.bfloat16)
        .at[:blocks]
        .set(jnp.broadcast_to(offsets[:, None], (blocks, atom_width)).astype(jnp.bfloat16))
    )
    packed = jnp.concatenate([atom_feats, offset_rows], axis=0)
    prev1, next1 = (shifted(packed, 1), shifted(packed, -1))
    prev2, next2 = (shifted(atom_feats[32:], 2), shifted(atom_feats[:32], -2))
    token_ends = jnp.cumsum(atom_counts, dtype=jnp.int32)
    token_starts = token_ends - atom_counts
    edges = atom_rows * jnp.arange(devices + 1, dtype=jnp.int32)
    bases = jnp.sum((token_starts[None, :] < edges[:, None]).astype(jnp.int32), axis=1)
    base = lax.dynamic_index_in_dim(bases, position, 0, keepdims=False)
    pad = jnp.full((16,), total_atoms, jnp.int32)
    padded_starts = jnp.concatenate([jnp.zeros((1,), jnp.int32) - MOST, token_starts, pad])
    padded_ends = jnp.concatenate([jnp.zeros((1,), jnp.int32), token_ends, pad])
    low = lax.dynamic_slice_in_dim(padded_starts, base, 16, 0)[:, None]
    high = lax.dynamic_slice_in_dim(padded_ends, base, 16, 0)[:, None]
    ext = jnp.concatenate([prev2, prev1[:64], atom_feats, next1[:64], next2], axis=0)
    feats_q = jnp.concatenate([prev1[32:64], atom_feats, next1[:32]], axis=0)
    off4 = jnp.concatenate([prev1[65:66, :1], offset_rows[0:2, :1], next1[64:65, :1]], axis=0)
    starts4 = (
        off4.astype(jnp.int32)
        + first_atom
        - QB
        - KW // 2
        + QB * jnp.arange(4, dtype=jnp.int32)[:, None]
    )
    starts = jnp.repeat(starts4, QB, axis=0)
    atom_out, single = atom_part(
        ext,
        feats_q,
        starts,
        first_atom,
        total_atoms,
        (low, high),
        atom_gain,
        w_query,
        w_key,
        w_value,
        w_out,
        w_pool,
        w_back,
    )
    slots = atom_rows // FEWEST
    slot_single = single[1 : 1 + slots]
    slot_index = jnp.arange(slots, dtype=jnp.int32)[None, :]
    token_id = jnp.where(
        slot_index < (bases[1:] - bases[:-1])[:, None], bases[:-1, None] + slot_index, -1
    )
    row_slots = cols * slots
    row_single = lax.all_gather(slot_single, "col", axis=0, tiled=True)
    row_ids = lax.dynamic_slice_in_dim(token_id.reshape(rows, row_slots), row, 1, 0)
    lr = project(row_single, jnp.concatenate([w_left, w_right], axis=1))
    gathered = lax.all_gather(lr, "row", axis=0, tiled=True)
    opm = w_left.shape[1]
    row_tokens, col_tokens, pair_width = pair_state.shape
    all_ids = token_id.reshape(1, -1)
    want_left = row * row_tokens + jnp.arange(row_tokens, dtype=jnp.int32)[:, None]
    want_right = col * col_tokens + jnp.arange(col_tokens, dtype=jnp.int32)[:, None]
    left_rows = project((all_ids == want_left).astype(jnp.bfloat16), gathered[:, :opm])
    right_cols = project((all_ids == want_right).astype(jnp.bfloat16), gathered[:, opm:])
    own = total_tokens // devices
    place = jnp.arange(rows * own, dtype=jnp.int32)
    want_own = (place // own * cols + col) * own + place % own
    spread = project((row_ids == want_own[:, None]).astype(jnp.bfloat16), row_single)
    token_single = lax.psum_scatter(spread, "row", scatter_dimension=0, tiled=True)
    outer_table = jnp.einsum(
        "jb,abc->jac", right_cols, w_outer, preferred_element_type=jnp.float32
    ).astype(jnp.bfloat16)
    step_rows = math.gcd(row_tokens, 8)

    def pair_block(pieces):
        left_block, pair_piece = pieces
        outer_term = jnp.einsum(
            "ia,jac->ijc", left_block, outer_table, preferred_element_type=jnp.float32
        )
        summed = pair_piece.astype(jnp.float32) + outer_term
        normed_pair = layer_norm(summed, pair_gain).astype(jnp.bfloat16)
        gate_proj = jnp.einsum(
            "ijc,cf->ijf", normed_pair, w_gate, preferred_element_type=jnp.float32
        )
        lift_proj = jnp.einsum(
            "ijc,cf->ijf", normed_pair, w_lift, preferred_element_type=jnp.float32
        )
        hidden = (jax.nn.silu(gate_proj) * lift_proj).astype(jnp.bfloat16)
        return (
            summed + jnp.einsum("ijf,fc->ijc", hidden, w_drop, preferred_element_type=jnp.float32)
        ).astype(jnp.bfloat16)

    pair_out = lax.map(
        pair_block,
        (
            left_rows.reshape(-1, step_rows, left_rows.shape[1]),
            pair_state.reshape(-1, step_rows, col_tokens, pair_width),
        ),
    )
    return (atom_out, token_single, pair_out.reshape(row_tokens, col_tokens, pair_width))


def solution(mesh):
    whole = P(BOTH, None)
    in_specs = (whole, P(BOTH)) + (P(),) * 8 + (P("row", "col", None),) + (P(),) * 7
    out_specs = (whole, whole, P("row", "col", None))
    return jax.shard_map(
        per_device, mesh=mesh, in_specs=in_specs, out_specs=out_specs, check_vma=False
    )
```

profile of v0, /device:TPU:2, one launch (start us, length us, event | category | flops | bytes accessed | tf_op | source)
XLA Modules:
  0.0 333.0 jit_solution(10406786678176366872)
XLA Ops:
  8.0 0.8 pad_maximum_fusion
  8.8 1.9 collective-permute-start.1
  10.7 2.4 collective-permute-start
  13.8 7.8 %collective-permute-start.3 = (bf16[32,128]{1,0:T(8,128)(2,1)S(1)}, bf16[32,128]{1,0:T(8,128)(2,1)S(1)}, u32[]{:S(2)}, u32[]{:S(2)}) collective-permute-start(bf16[32,128]{1,0:T(8,128)(2,1)S(1)} %get-tuple-element.133), channel_id=1, source_target_pairs={{2,0},{3,1},{4,2},{5,3},{6,4},{7,5},{8,6},{9,7},{10,8},{11,9},{12,... | collective-permute-start | bytes 24584 | tf_op jit(solution)/shard_map/ppermute | solution.py:19
  21.6 1.9 collective-permute-start.2
  23.6 1.0 reduce-window.9
  24.8 0.8 fusion.93
  30.2 1.3 dynamic-slice.6
  33.2 1.4 fusion.89
  35.8 0.8 fusion.47
  36.6 1.0 convolution_convert_fusion.4
  37.6 1.0 convolution_convert_fusion.3
  41.5 21.2 %all_gather.6 = bf16[128,384]{1,0:T(8,128)(2,1)S(1)} all-gather(bf16[8,384]{1,0:T(8,128)(2,1)S(1)} %slice.169), channel_id=1, replica_groups=mesh['row'=32,'col'=16] {'col'}, dimensions={0}, use_global_device_ids=true | all-gather | bytes 104448 | tf_op jit(solution)/shard_map/all_gather | solution.py:177
  62.7 0.9 convolution_convert_fusion.1
  63.8 72.7 %all_gather.7 = bf16[4096,64]{0,1:T(8,128)(2,1)S(1)} all-gather(bf16[128,64]{0,1:T(8,128)(2,1)S(1)} %convolution_convert_fusion.5), channel_id=1, replica_groups=mesh['row'=32,'col'=16] {'row'}, dimensions={0}, use_global_device_ids=true | all-gather | bytes 540672 | tf_op jit(solution)/shard_map/all_gather | solution.py:180
  136.9 1.4 convolution_convert_fusion
  139.1 37.6 %while.11 = (s32[]{:T(128)}, bf16[8,8,128,128]{3,2,1,0:T(8,128)(2,1)}, bf16[8,8,128,128]{3,2,1,0:T(8,128)(2,1)}, bf16[8,8,32]{2,1,0:T(8,128)(2,1)S(1)}, bf16[128...) while((s32[]{:T(128)}, ...), condition=%wide.region_13.14_spmd, body=%wide.region_10.13_spmd.sunk | while | flops 415761408 | bytes 12229241 | solution.py:216
  139.1 1.0 constant_dynamic-slice_fusion.3
  143.9 1.0 constant_dynamic-slice_fusion.3
  147.8 0.7 copy_dynamic-update-slice_fusion.2
  148.5 1.0 constant_dynamic-slice_fusion.3
  152.5 0.7 copy_dynamic-update-slice_fusion.2
  153.2 1.0 constant_dynamic-slice_fusion.3
  157.2 0.7 copy_dynamic-update-slice_fusion.2
  157.9 1.0 constant_dynamic-slice_fusion.3
  161.9 0.7 copy_dynamic-update-slice_fusion.2
  162.6 1.0 constant_dynamic-slice_fusion.3
  167.3 1.0 constant_dynamic-slice_fusion.3
  172.0 1.0 constant_dynamic-slice_fusion.3
  176.7 0.9 fusion.24
  177.6 147.3 %all-reduce.4.cloned.1.call-done = bf16[128,384]{1,0:T(8,128)(2,1)} async-done(((bf16[128,384]{1,0:T(8,128)(2,1)}), bf16[128,384]{1,0:T(8,128)(2,1)}) %all-reduce.4.cloned.1.call-update) | async-done | bytes 98320
  324.9 1.3 constant_dynamic-slice_fusion.1
  (167 shorter events, 37.1 us)
Async XLA Ops:
  7.2 129.8 %copy-start = (bf16[32,32,128]{2,1,0:T(8,128)(2,1)S(1)}, bf16[32,32,128]{2,1,0:T(8,128)(2,1)}, u32[]{:S(2)}) copy-start(bf16[32,32,128]{2,1,0:T(8,128)(2,1)} %param.35) | copy-start | bytes 786436
  7.2 32.6 %copy-start.5 = (bf16[128,128]{1,0:T(8,128)(2,1)S(1)}, bf16[128,128]{1,0:T(8,128)(2,1)}, u32[]{:S(2)}) copy-start(bf16[128,128]{1,0:T(8,128)(2,1)} %param.28) | copy-start | bytes 98308
  7.2 317.7 %all-reduce.4.cloned.1.call-start = ((), (), s32[]{:S(2)}) async-start(), calls=%async_computation | async-start | bytes 196608
  8.8 23.4 %collective-permute-start.1 = (bf16[72,128]{1,0:T(8,128)(2,1)S(1)}, bf16[72,128]{1,0:T(8,128)(2,1)S(1)}, u32[]{:S(2)}, u32[]{:S(2)}) collective-permute-start(bf16[72,128]{1,0:T(8,128)(2,1)S(1)} %pad_maximum_fusion), channel_id=1, source_target_pairs={{1,0},{2,1},{3,2},{4,3},{5,4},{6,5},{7,6},{8,7},{9,8},{10,9},{11,1... | collective-permute-start | bytes 55304 | tf_op jit(solution)/shard_map/ppermute | solution.py:19
  10.7 22.0 %collective-permute-start = (bf16[72,128]{1,0:T(8,128)(2,1)S(1)}, bf16[72,128]{1,0:T(8,128)(2,1)S(1)}, u32[]{:S(2)}, u32[]{:S(2)}) collective-permute-start(bf16[72,128]{1,0:T(8,128)(2,1)S(1)} %pad_maximum_fusion), channel_id=1, source_target_pairs={{0,1},{1,2},{2,3},{3,4},{4,5},{5,6},{6,7},{7,8},{8,9},{9,10},{10,1... | collective-permute-start | bytes 55304 | tf_op jit(solution)/shard_map/ppermute | solution.py:19
  13.8 21.6 %collective-permute-start.3 = (bf16[32,128]{1,0:T(8,128)(2,1)S(1)}, bf16[32,128]{1,0:T(8,128)(2,1)S(1)}, u32[]{:S(2)}, u32[]{:S(2)}) collective-permute-start(bf16[32,128]{1,0:T(8,128)(2,1)S(1)} %get-tuple-element.133), channel_id=1, source_target_pairs={{2,0},{3,1},{4,2},{5,3},{6,4},{7,5},{8,6},{9,7},{10,8},{11,9},{12,... | collective-permute-start | bytes 24584 | tf_op jit(solution)/shard_map/ppermute | solution.py:19
  21.6 10.5 %collective-permute-start.2 = (bf16[32,128]{1,0:T(8,128)(2,1)S(1)}, bf16[32,128]{1,0:T(8,128)(2,1)S(1)}, u32[]{:S(2)}, u32[]{:S(2)}) collective-permute-start(bf16[32,128]{1,0:T(8,128)(2,1)S(1)} %get-tuple-element.134), channel_id=1, source_target_pairs={{0,2},{1,3},{2,4},{3,5},{4,6},{5,7},{6,8},{7,9},{8,10},{9,11},{10,... | collective-permute-start | bytes 24584 | tf_op jit(solution)/shard_map/ppermute | solution.py:19
  32.1 8.9 %copy-start.3 = (bf16[64,128]{1,0:T(8,128)(2,1)S(1)}, bf16[64,128]{1,0:T(8,128)(2,1)}, u32[]{:S(2)}) copy-start(bf16[64,128]{1,0:T(8,128)(2,1)} %param.22) | copy-start | bytes 49156
  32.1 8.9 %copy-start.11 = (bf16[128,128]{1,0:T(8,128)(2,1)S(1)}, bf16[128,128]{1,0:T(8,128)(2,1)}, u32[]{:S(2)}) copy-start(bf16[128,128]{1,0:T(8,128)(2,1)} %param.29) | copy-start | bytes 98308
  35.6 5.6 %copy-start.10 = (bf16[128,384]{1,0:T(8,128)(2,1)S(1)}, bf16[128,384]{1,0:T(8,128)(2,1)}, u32[]{:S(2)}) copy-start(bf16[128,384]{1,0:T(8,128)(2,1)} %param.30) | copy-start | bytes 294916
  38.9 24.7 %copy-start.6 = (bf16[384,32]{0,1:T(8,128)(2,1)S(1)}, bf16[384,32]{0,1:T(8,128)(2,1)}, u32[]{:S(2)}) copy-start(bf16[384,32]{0,1:T(8,128)(2,1)} %param.34) | copy-start | bytes 73732
  38.9 24.7 %copy-start.7 = (bf16[384,32]{0,1:T(8,128)(2,1)S(1)}, bf16[384,32]{0,1:T(8,128)(2,1)}, u32[]{:S(2)}) copy-start(bf16[384,32]{0,1:T(8,128)(2,1)} %param.33) | copy-start | bytes 73732
  136.4 2.6 copy-start.1
  136.4 2.6 copy-start.2
  136.4 2.6 copy-start.8
  136.4 2.7 copy-start.9
  139.1 37.6 %copy-start.4 = (bf16[384,128]{1,0:T(8,128)(2,1)S(1)}, bf16[384,128]{1,0:T(8,128)(2,1)}, u32[]{:S(2)}) copy-start(bf16[384,128]{1,0:T(8,128)(2,1)} %param.31) | copy-start | bytes 294916
Sparse Core Ops, SparseCore 0:
  63.7 261.1 all-reduce.3
where the time goes:
time: 334 us; the launch traced here: 333 us
  waiting for transfers between devices  147 us (44%)
  blocking collectives  93.9 us (28%)
  matrix products  26.1 us (8%)
  local copies, waits for them, and re-layouts  21.3 us (6%)
  between operations  17.1 us (5%)
  starting transfers between devices  14.1 us (4%)
  other arithmetic  12.9 us (4%)
    unnamed x2, waiting for transfers between devices  147 us
    all_gather x1, blocking collectives, per_device(): gathered = lax.all_gather(lr, 'row', axis=0, tiled=True)  72.7 us
    all_gather x1, blocking collectives, per_device(): row_single = lax.all_gather(slot_single, 'col', axis=0, tiled=True)  21.2 us
    ppermute x4, starting transfers between devices, shifted(): return lax.ppermute(block, BOTH, route)  14 us
    dynamic_slice x8, local copies, waits for them, and re-layouts, per_device(): lax.map(pair_block, (left_rows.reshape(-1, step_rows, left_rows.shape[1])...  7.78 us
  transfers between devices with their start and end apart: 5, of which 1 were waited for; matrix products, arithmetic and copies ran while one was open for 15% of the time, Pallas kernels for 0%

commit v1 on v0

--- a/solution.py
+++ b/solution.py
@@ -11,6 +11,12 @@
 MOST = 24
 EPSILON = 1e-05
 BOTH = ("row", "col")
+
+
+def _derive_ends(u, along_axis):
+    return jnp.concatenate(
+        jax.lax.all_to_all(jnp.stack([u] * jax.lax.axis_size(along_axis)), along_axis, 0, 0), 0
+    )
 
 
 def shifted(block, distance):
@@ -177,7 +183,7 @@
     row_single = lax.all_gather(slot_single, "col", axis=0, tiled=True)
     row_ids = lax.dynamic_slice_in_dim(token_id.reshape(rows, row_slots), row, 1, 0)
     lr = project(row_single, jnp.concatenate([w_left, w_right], axis=1))
-    gathered = lax.all_gather(lr, "row", axis=0, tiled=True)
+    gathered = _derive_ends(lr, "row")
     opm = w_left.shape[1]
     row_tokens, col_tokens, pair_width = pair_state.shape
     all_ids = token_id.reshape(1, -1)

time: 334 us -> 388 us (1.16)
  waiting for transfers between devices: 147 us -> 253 us
  blocking collectives: 93.9 us -> 21.2 us
  starting transfers between devices: 14.1 us -> 34.1 us
    unnamed x2, waiting for transfers between devices: 147 us -> 253 us
    all_gather x1 -> x0, blocking collectives: 72.7 us -> none  [per_device(): gathered = lax.all_gather(lr, 'row', axis=0, tiled=True)]
    all_to_all x0 -> x1, starting transfers between devices: none -> 20 us  [_derive_ends(): jax.lax.all_to_all(jnp.stack([u] * jax.lax.axis_size(along_axis)), along_...]
  transfers between devices with their start and end apart: 5 -> 6, of which waited for: 1 -> 1; matrix products, arithmetic and copies ran while one was open for 15% -> 3% of each run, Pallas kernels for 0% -> 0%
where the time goes in v1:
time: 388 us; the launch traced here: 387 us
  waiting for transfers between devices  253 us (65%)
  starting transfers between devices  34.1 us (9%)
  matrix products  26.2 us (7%)
  local copies, waits for them, and re-layouts  22.2 us (6%)
  blocking collectives  21.2 us (5%)
  between operations  17.1 us (4%)
  other arithmetic  12.9 us (3%)
    unnamed x2, waiting for transfers between devices  253 us
    all_gather x1, blocking collectives, per_device(): row_single = lax.all_gather(slot_single, 'col', axis=0, tiled=True)  21.2 us
    all_to_all x1, starting transfers between devices, _derive_ends(): jax.lax.all_to_all(jnp.stack([u] * jax.lax.axis_size(along_axis)), along_...  20 us
    ppermute x4, starting transfers between devices, shifted(): return lax.ppermute(block, BOTH, route)  14 us
  transfers between devices with their start and end apart: 6, of which 1 were waited for; matrix products, arithmetic and copies ran while one was open for 3% of the time, Pallas kernels for 0%

profile of v1, /device:TPU:2, one launch (start us, length us, event | category | flops | bytes accessed | tf_op | source)
XLA Modules:
  0.0 387.3 jit_solution(17821790177145892687)
XLA Ops:
  8.0 0.8 pad_maximum_fusion
  8.8 1.9 collective-permute-start.1
  10.7 2.4 collective-permute-start
  13.8 7.8 %collective-permute-start.3 = (bf16[32,128]{1,0:T(8,128)(2,1)S(1)}, bf16[32,128]{1,0:T(8,128)(2,1)S(1)}, u32[]{:S(2)}, u32[]{:S(2)}) collective-permute-start(bf16[32,128]{1,0:T(8,128)(2,1)S(1)} %get-tuple-element.142), channel_id=1, source_target_pairs={{2,0},{3,1},{4,2},{5,3},{6,4},{7,5},{8,6},{9,7},{10,8},{11,9},{12,... | collective-permute-start | bytes 24584 | tf_op jit(solution)/shard_map/ppermute | solution.py:25
  21.6 1.9 collective-permute-start.2
  23.6 1.0 reduce-window.9
  24.8 0.8 fusion.93
  30.0 1.4 fusion.89
  32.6 0.8 fusion.47
  33.4 1.0 convolution_convert_fusion.4
  34.4 1.0 convolution_convert_fusion.3
  38.3 21.2 %all_gather.3 = bf16[128,384]{1,0:T(8,128)(2,1)S(1)} all-gather(bf16[8,384]{1,0:T(8,128)(2,1)S(1)} %slice.169), channel_id=1, replica_groups=mesh['row'=32,'col'=16] {'col'}, dimensions={0}, use_global_device_ids=true | all-gather | bytes 104448 | tf_op jit(solution)/shard_map/all_gather | solution.py:183
  59.7 0.9 stack.2
  60.6 20.0 %all-to-all-start = ((bf16[32,128,64]{1,2,0:T(8,128)(2,1)}), bf16[32,128,64]{1,2,0:T(8,128)(2,1)S(1)}, u32[]{:S(2)}, u32[]{:S(2)}) async-start(bf16[32,128,64]{1,2,0:T(8,128)(2,1)} %stack.2), calls=%async_computation | async-start | bytes 1048576 | tf_op jit(solution)/shard_map/all_to_all | solution.py:18
  81.6 1.3 dynamic-slice.6
  83.9 0.9 convolution_convert_fusion.1
  84.8 0.9 fusion.24
  85.6 253.1 %all-reduce.4.cloned.1.call-done = bf16[128,384]{1,0:T(8,128)(2,1)} async-done(((bf16[128,384]{1,0:T(8,128)(2,1)}), bf16[128,384]{1,0:T(8,128)(2,1)}) %all-reduce.4.cloned.1.call-update) | async-done | bytes 98320
  338.8 1.3 constant_dynamic-slice_fusion.1
  340.6 1.4 convolution_convert_fusion
  342.8 37.7 %while.11 = (s32[]{:T(128)}, bf16[8,8,128,128]{3,2,1,0:T(8,128)(2,1)}, bf16[8,8,128,128]{3,2,1,0:T(8,128)(2,1)}, bf16[8,8,32]{2,1,0:T(8,128)(2,1)S(1)}, bf16[128...) while((s32[]{:T(128)}, ...), condition=%wide.region_13.14_spmd, body=%wide.region_10.13_spmd.sunk | while | flops 415761408 | bytes 12229241 | solution.py:222
  342.8 1.0 constant_dynamic-slice_fusion.3
  346.8 0.7 copy_dynamic-update-slice_fusion.2
  347.5 1.0 constant_dynamic-slice_fusion.3
  351.5 0.7 copy_dynamic-update-slice_fusion.2
  352.3 1.0 constant_dynamic-slice_fusion.3
  356.2 0.7 copy_dynamic-update-slice_fusion.2
  357.0 1.0 constant_dynamic-slice_fusion.3
  361.7 1.0 constant_dynamic-slice_fusion.3
  366.4 1.0 constant_dynamic-slice_fusion.3
  371.1 1.0 constant_dynamic-slice_fusion.3
  375.8 1.0 constant_dynamic-slice_fusion.3
  (170 shorter events, 38.1 us)
Async XLA Ops:
  7.2 333.5 %copy-start = (bf16[32,32,128]{2,1,0:T(8,128)(2,1)S(1)}, bf16[32,32,128]{2,1,0:T(8,128)(2,1)}, u32[]{:S(2)}) copy-start(bf16[32,32,128]{2,1,0:T(8,128)(2,1)} %param.35) | copy-start | bytes 786436
  7.2 29.4 %copy-start.5 = (bf16[128,128]{1,0:T(8,128)(2,1)S(1)}, bf16[128,128]{1,0:T(8,128)(2,1)}, u32[]{:S(2)}) copy-start(bf16[128,128]{1,0:T(8,128)(2,1)} %param.28) | copy-start | bytes 98308
  8.8 20.2 %collective-permute-start.1 = (bf16[72,128]{1,0:T(8,128)(2,1)S(1)}, bf16[72,128]{1,0:T(8,128)(2,1)S(1)}, u32[]{:S(2)}, u32[]{:S(2)}) collective-permute-start(bf16[72,128]{1,0:T(8,128)(2,1)S(1)} %pad_maximum_fusion), channel_id=1, source_target_pairs={{1,0},{2,1},{3,2},{4,3},{5,4},{6,5},{7,6},{8,7},{9,8},{10,9},{11,1... | collective-permute-start | bytes 55304 | tf_op jit(solution)/shard_map/ppermute | solution.py:25
  10.7 18.8 %collective-permute-start = (bf16[72,128]{1,0:T(8,128)(2,1)S(1)}, bf16[72,128]{1,0:T(8,128)(2,1)S(1)}, u32[]{:S(2)}, u32[]{:S(2)}) collective-permute-start(bf16[72,128]{1,0:T(8,128)(2,1)S(1)} %pad_maximum_fusion), channel_id=1, source_target_pairs={{0,1},{1,2},{2,3},{3,4},{4,5},{5,6},{6,7},{7,8},{8,9},{9,10},{10,1... | collective-permute-start | bytes 55304 | tf_op jit(solution)/shard_map/ppermute | solution.py:25
  13.8 18.5 %collective-permute-start.3 = (bf16[32,128]{1,0:T(8,128)(2,1)S(1)}, bf16[32,128]{1,0:T(8,128)(2,1)S(1)}, u32[]{:S(2)}, u32[]{:S(2)}) collective-permute-start(bf16[32,128]{1,0:T(8,128)(2,1)S(1)} %get-tuple-element.142), channel_id=1, source_target_pairs={{2,0},{3,1},{4,2},{5,3},{6,4},{7,5},{8,6},{9,7},{10,8},{11,9},{12,... | collective-permute-start | bytes 24584 | tf_op jit(solution)/shard_map/ppermute | solution.py:25
  21.6 7.3 %collective-permute-start.2 = (bf16[32,128]{1,0:T(8,128)(2,1)S(1)}, bf16[32,128]{1,0:T(8,128)(2,1)S(1)}, u32[]{:S(2)}, u32[]{:S(2)}) collective-permute-start(bf16[32,128]{1,0:T(8,128)(2,1)S(1)} %get-tuple-element.143), channel_id=1, source_target_pairs={{0,2},{1,3},{2,4},{3,5},{4,6},{5,7},{6,8},{7,9},{8,10},{9,11},{10,... | collective-permute-start | bytes 24584 | tf_op jit(solution)/shard_map/ppermute | solution.py:25
  28.9 8.9 %copy-start.3 = (bf16[64,128]{1,0:T(8,128)(2,1)S(1)}, bf16[64,128]{1,0:T(8,128)(2,1)}, u32[]{:S(2)}) copy-start(bf16[64,128]{1,0:T(8,128)(2,1)} %param.22) | copy-start | bytes 49156
  28.9 8.9 %copy-start.11 = (bf16[128,128]{1,0:T(8,128)(2,1)S(1)}, bf16[128,128]{1,0:T(8,128)(2,1)}, u32[]{:S(2)}) copy-start(bf16[128,128]{1,0:T(8,128)(2,1)} %param.29) | copy-start | bytes 98308
  32.4 5.6 %copy-start.10 = (bf16[128,384]{1,0:T(8,128)(2,1)S(1)}, bf16[128,384]{1,0:T(8,128)(2,1)}, u32[]{:S(2)}) copy-start(bf16[128,384]{1,0:T(8,128)(2,1)} %param.30) | copy-start | bytes 294916
  35.4 24.2 %copy-start.6 = (bf16[384,32]{0,1:T(8,128)(2,1)S(1)}, bf16[384,32]{0,1:T(8,128)(2,1)}, u32[]{:S(2)}) copy-start(bf16[384,32]{0,1:T(8,128)(2,1)} %param.34) | copy-start | bytes 73732
  35.4 24.1 %copy-start.7 = (bf16[384,32]{0,1:T(8,128)(2,1)S(1)}, bf16[384,32]{0,1:T(8,128)(2,1)}, u32[]{:S(2)}) copy-start(bf16[384,32]{0,1:T(8,128)(2,1)} %param.33) | copy-start | bytes 73732
  37.6 47.2 %copy-start.4 = (bf16[384,128]{1,0:T(8,128)(2,1)S(1)}, bf16[384,128]{1,0:T(8,128)(2,1)}, u32[]{:S(2)}) copy-start(bf16[384,128]{1,0:T(8,128)(2,1)} %param.31) | copy-start | bytes 294916
  60.6 279.4 %all-to-all-start = ((bf16[32,128,64]{1,2,0:T(8,128)(2,1)}), bf16[32,128,64]{1,2,0:T(8,128)(2,1)S(1)}, u32[]{:S(2)}, u32[]{:S(2)}) async-start(bf16[32,128,64]{1,2,0:T(8,128)(2,1)} %stack.2), calls=%async_computation | async-start | bytes 1048576 | tf_op jit(solution)/shard_map/all_to_all | solution.py:18
  80.7 258.1 %all-reduce.4.cloned.1.call-start = ((), (), s32[]{:S(2)}) async-start(), calls=%async_computation.1 | async-start | bytes 196608
  340.1 2.7 copy-start.1
  340.1 2.7 copy-start.2
  340.1 2.7 copy-start.8
  340.2 2.7 copy-start.9
Sparse Core Ops, SparseCore 0:
  84.9 253.8 all-reduce.3
